TPU v7x, 256 devices: a whole 4x4x8 slice. The times are simulated.
256 devices in a mesh: build: 2 (over y_lo), test: 8 (over x, core), stmt: 16 (over y_hi, z).
Axes of the slice: x: 4, y: 4 (y_hi: 2, y_lo: 2; y = y_hi * 2 + y_lo), z: 8, core: 2. Of those that a mesh axis runs over, the one named last changes fastest.
Arguments:
- tile_values: bfloat16 [2, 8, 16, 2, 128, 128, 128], P('build', 'test', 'stmt'), may hold values from -6 to 6
- tile_test: int32 [2, 8, 16, 2], P('build', 'test', 'stmt'), may hold values from 0 to 3, as said below
- tile_stmt: int32 [2, 8, 16, 2], P('build', 'test', 'stmt'), may hold values from 0 to 1, as said below
- tile_build: int32 [2, 8, 16, 2], P('build', 'test', 'stmt'), may hold values from 0 to 5, as said below
- tile_count: int32 [2, 8, 16], P('build', 'test', 'stmt'), may hold values from 0 to 2, as said below
- test_factor: bfloat16 [8, 512, 256], P('test', ('build', 'stmt')), may hold values from -0.027063294 to 0.027063294
- build_factor: bfloat16 [2, 768, 256], P('build', ('test', 'stmt')), may hold values from -0.027063294 to 0.027063294
Outputs:
- stmt_factor: float32 [16, 256, 256], P('stmt', ('build', 'test'))
Inputs may be any that keep to these rules, and one draw needn't show every extreme that they name: `tile_count`: slots from this count on hold padding: their values and block numbers must not contribute. Some grid position has every slot live and some has none. `tile_test`: test block of a slot; the largest block is named in every draw. `tile_stmt`: statement block of a slot; the largest block is named in every draw. `tile_build`: build block of a slot; the largest block is named in every draw.
All inputs are finite; a program needn't handle non-finite values.
Results may differ from a plain program's by a relative error of at most 0.003.
Values may be sent and summed in bfloat16 or wider, within the bound.
A program may use at most 64 MiB of HBM per device.

v0:
```python
import jax
import jax.numpy as jnp
from jax import lax
from jax.sharding import PartitionSpec as P

TILE = 128
SB = 2
ALL = ("build", "test", "stmt")


def shards(tile_values, tile_test, tile_stmt, tile_build, tile_count, test_factor, build_factor):
    test_rows = test_factor[0]
    build_rows = build_factor[0]
    local_grams = jnp.stack(
        [
            lax.dot_general(
                test_rows, test_rows, (((0,), (0,)), ((), ())), preferred_element_type=jnp.float32
            ),
            lax.dot_general(
                build_rows, build_rows, (((0,), (0,)), ((), ())), preferred_element_type=jnp.float32
            ),
        ]
    )
    grams = lax.psum(local_grams, ALL)
    gram = grams[0] * grams[1]
    lower = jnp.linalg.cholesky(gram)
    test_slab = lax.all_gather(test_rows, ("build", "stmt"), axis=0, tiled=True)
    build_slab = lax.all_gather(build_rows, ("test", "stmt"), axis=0, tiled=True)
    slot_values = tile_values[0, 0, 0]
    slot_tests = tile_test[0, 0, 0]
    slot_stmts = tile_stmt[0, 0, 0]
    slot_builds = tile_build[0, 0, 0]
    live_count = tile_count[0, 0, 0]
    tile_width = slot_values.shape[-1]
    rank_width = test_slab.shape[1]
    running_sum = jnp.zeros((SB * TILE, rank_width), jnp.float32)
    for slot_index in range(slot_values.shape[0]):
        test_block = lax.dynamic_slice_in_dim(
            test_slab, slot_tests[slot_index] * tile_width, tile_width, 0
        ).astype(jnp.float32)
        build_block = lax.dynamic_slice_in_dim(
            build_slab, slot_builds[slot_index] * tile_width, tile_width, 0
        ).astype(jnp.float32)
        khatri_rao = (test_block[:, None, :] * build_block[None, :, :]).astype(jnp.bfloat16)
        term = jnp.einsum(
            "ijk,ikr->jr", slot_values[slot_index], khatri_rao, preferred_element_type=jnp.float32
        )
        live_weight = (slot_index < live_count).astype(jnp.float32)
        accumulate_term = term * live_weight
        start_row = slot_stmts[slot_index] * tile_width
        current = lax.dynamic_slice_in_dim(running_sum, start_row, tile_width, 0)
        running_sum = lax.dynamic_update_slice_in_dim(
            running_sum, current + accumulate_term, start_row, 0
        )
    owned_sums = lax.psum_scatter(running_sum, ("build", "test"), scatter_dimension=0, tiled=True)
    halfway = lax.linalg.triangular_solve(
        lower, owned_sums, left_side=False, lower=True, transpose_a=True
    )
    solved = lax.linalg.triangular_solve(
        lower, halfway, left_side=False, lower=True, transpose_a=False
    )
    return solved[None]


def solution(mesh):
    return jax.shard_map(
        shards,
        mesh=mesh,
        in_specs=(
            P("build", "test", "stmt", None, None, None, None),
            P("build", "test", "stmt", None),
            P("build", "test", "stmt", None),
            P("build", "test", "stmt", None),
            P("build", "test", "stmt"),
            P("test", ("build", "stmt"), None),
            P("build", ("test", "stmt"), None),
        ),
        out_specs=P("stmt", ("build", "test"), None),
        check_vma=False,
    )
```

profile of v0, /device:TPU:32, one launch (start us, length us, event | category | flops | bytes accessed | tf_op | source)
XLA Modules:
  0.0 509.7 jit_solution(10829243908084318337)
XLA Ops:
  7.4 0.0 all-reduce.3.cloned.1.call-start
  7.4 1.0 convolution_bitcast_fusion
  8.4 1.0 convolution_bitcast_fusion.1
  9.4 0.8 pad_maximum_fusion
  10.2 0.0 all-reduce.3.cloned.1.call-update
  10.2 0.0 reduce-scatter.2.cloned.1.call-start
  10.3 1.3 fusion.53
  12.9 0.7 copy.15
  13.6 1.3 fusion.52
  16.2 73.7 %all-gather = bf16[1,512,256]{2,1,0:T(8,128)(2,1)S(1)} all-gather(bf16[1,16,256]{2,1,0:T(8,128)(2,1)} %param.12), channel_id=2, replica_groups=mesh['build'=2,'test'=8,'stmt'=16] {'build','stmt'}, dimensions={1}, use_global_device_ids=true | all-gather | bytes 270336 | tf_op jit(solution)/shard_map/all_gather | solution.py:27
  89.9 1.3 fusion.54
  92.5 328.3 %all-gather.1 = bf16[1,768,256]{2,0,1:T(2,128)(2,1)S(1)} all-gather(bf16[1,6,256]{2,0,1:T(2,128)(2,1)S(1)} %copy.15), channel_id=3, replica_groups=mesh['build'=2,'test'=8,'stmt'=16] {'test','stmt'}, dimensions={1}, use_global_device_ids=true | all-gather | bytes 396288 | tf_op jit(solution)/shard_map/all_gather | solution.py:28
  420.8 0.3 dynamic-slice_convert_fusion
  421.1 0.1 copy.27
  421.8 0.1 copy.29
  422.0 0.0 slice-start
  422.0 0.0 slice-start.1
  422.0 9.1 %fusion.28 = f32[256,256]{1,0:T(8,128)S(1)} fusion(f32[256,256]{1,0:T(8,128)S(1)} %broadcast_in_dim.6, s32[]{:T(128)S(6)} %select_n.25, bf16[1,1,1,2,128,128,128]{6,5,4,3,2,1,0:T(8,128)(2,1)} %param.7, f32[128,256]{0,1:T(8,128)S(1)} %bitcast.119, f32[128,256]{1,0:T(8,128)S(1)} %get-tuple-element.26, f32[]{:T(128)} %bitcast.6), kind=kOutput, calls=%fused_computation.22 | convolution fusion | flops 1082163200 | bytes 4588036 | tf_op jit(solution)/shard_map/ijk,ikr->jr/dot_general | solution.py:45
  431.2 0.0 slice-done
  431.2 0.0 slice-done.1
  431.2 5.3 %fusion.34 = f32[256,256]{1,0:T(8,128)S(1)} fusion(f32[256,256]{1,0:T(8,128)S(1)} %fusion.28, s32[]{:T(128)S(6)} %select_n.26, bf16[1,1,1,2,128,128,128]{6,5,4,3,2,1,0:T(8,128)(2,1)S(1)} %bitcast.122, f32[128,256]{0,1:T(8,128)S(1)} %bitcast.120, f32[128,256]{1,0:T(8,128)S(1)} %get-tuple-element.25, f32[]{:T(128)} %bitcast.16), kind=kOutput, calls=%fused_computation.24 | convolution fusion | flops 1082195968 | bytes 4718600 | tf_op jit(solution)/shard_map/ijk,ikr->jr/dot_general | solution.py:45
  436.5 0.0 copy-start
  436.5 0.7 copy-done
  437.2 0.0 reduce-scatter.2.cloned.1.call-update
  437.2 0.0 all-reduce.3.cloned.1.call-done
  437.2 1.1 fusion.38
  438.3 0.1 copy.22
  438.4 1.1 fusion.37
  439.5 11.7 %cholesky.49 = f32[128,128]{1,0:T(8,128)S(1)} custom-call(f32[128,128]{1,0:T(8,128)S(1)} %cholesky.115), custom_call_target="Cholesky" | custom-call | tf_op jit(solution)/shard_map/jit(cholesky)/cholesky | solution.py:26
  451.3 9.8 %custom-call.16 = f32[1,128,128]{1,2,0:T(8,128)S(1)} custom-call(f32[1,128,128]{2,1,0:T(8,128)S(1)} %get-tuple-element.30), custom_call_target="InvertDiagBlocksLowerTriangular" | custom-call | tf_op jit(solution)/shard_map/jit(cholesky)/cholesky | solution.py:26
  461.1 0.2 constant_dynamic-update-slice_fusion
  461.3 0.3 convolution_subtract_fusion
  461.6 11.7 %cholesky.103 = f32[128,128]{1,0:T(8,128)S(1)} custom-call(f32[128,128]{1,0:T(8,128)S(1)} %convolution_subtract_fusion), custom_call_target="Cholesky" | custom-call | tf_op jit(solution)/shard_map/jit(cholesky)/cholesky | solution.py:26
  473.4 0.7 compare_reduce_fusion
  475.2 0.1 triangular_solve.67
  475.3 3.8 while.1
  475.3 0.6 fusion.63
  475.9 1.3 bitcast_dynamic-update-slice_fusion.2
  477.2 0.6 fusion.63
  477.8 1.3 bitcast_dynamic-update-slice_fusion.2
  479.1 19.9 %custom-call.17 = f32[2,128,128]{1,2,0:T(8,128)S(1)} custom-call(f32[2,128,128]{2,1,0:T(8,128)S(1)} %get-tuple-element.12), custom_call_target="InvertDiagBlocksLowerTriangular" | custom-call | tf_op jit(solution)/shard_map/triangular_solve | solution.py:56
  499.0 0.0 reduce-scatter.2.cloned.1.call-done
  499.0 0.8 fusion.43
  499.9 0.9 convolution_subtract_fusion.2
  500.8 0.2 fusion.45
  501.0 0.2 fusion.44
  501.2 0.2 convolution_subtract_fusion.1
  501.4 0.2 fusion.42
  501.6 0.7 maximum_bitcast_fusion
  (12 shorter events, 0.2 us)
Async XLA Ops:
  7.4 429.9 %all-reduce.3.cloned.1.call-start = ((), (), s32[]{:S(2)}) async-start(), calls=%async_computation.2 | async-start | bytes 1048576 | tf_op jit(solution)/shard_map/psum | solution.py:24
  10.2 488.8 %reduce-scatter.2.cloned.1.call-start = ((), (), s32[]{:S(2)}) async-start(), calls=%async_computation.1 | async-start | bytes 278528 | tf_op jit(solution)/shard_map/reduce_scatter | solution.py:55
  422.0 9.2 %slice-start = ((s8[8388608]{0:T(1024)(128)(4,1)}), s8[4194304]{0:T(1024)(128)(4,1)S(1)}, s32[]{:S(2)}) async-start(s8[8388608]{0:T(1024)(128)(4,1)} %bitcast.121), calls=%async_computation.3 | async-start | bytes 8388608
  422.0 9.2 %slice-start.1 = ((s8[8388608]{0:T(1024)(128)(4,1)}), s8[4194304]{0:T(1024)(128)(4,1)S(1)}, s32[]{:S(2)}) async-start(s8[8388608]{0:T(1024)(128)(4,1)} %bitcast.121), calls=%async_computation.4 | async-start | bytes 8388608
  436.5 0.7 copy-start
Sparse Core Ops, SparseCore 0:
  13.6 256.4 all-reduce.2
Sparse Core Ops, SparseCore 1:
  437.3 56.1 reduce-scatter.1
where the time goes:
time: 510 us
  blocking collectives  402 us (79%)
  other arithmetic  57.8 us (11%)
  between operations  20.7 us (4%)
  matrix products  19.4 us (4%)
  local copies, waits for them, and re-layouts  9.57 us (2%)
    all_gather x1, blocking collectives, shards(): lax.all_gather(build_rows, ('test', 'stmt'), axis=0, tiled=True)  328 us
    all_gather x1, blocking collectives, shards(): test_slab = lax.all_gather(test_rows, ('build', 'stmt'), axis=0, tiled=True)  73.7 us
    another operation x6, other arithmetic, shards(): lower = jnp.linalg.cholesky(gram)  34 us
    another operation x3, other arithmetic, shards(): lax.linalg.triangular_solve(lower, owned_sums, left_side=False, lower=Tru...  19.9 us
    dot_general x2, matrix products, shards(): jnp.einsum('ijk,ikr->jr', slot_values[slot_index], khatri_rao, preferred_...  14.4 us
  transfers between devices with their start and end apart: 2, of which 0 were waited for; matrix products, arithmetic and copies ran while one was open for 16% of the time, Pallas kernels for 0%

commit v1 on v0

--- a/solution.py
+++ b/solution.py
@@ -25,7 +25,12 @@
     gram = grams[0] * grams[1]
     lower = jnp.linalg.cholesky(gram)
     test_slab = lax.all_gather(test_rows, ("build", "stmt"), axis=0, tiled=True)
-    build_slab = lax.all_gather(build_rows, ("test", "stmt"), axis=0, tiled=True)
+    build_slab = jnp.concatenate(
+        lax.all_to_all(
+            jnp.stack([build_rows] * lax.axis_size(("test", "stmt"))), ("test", "stmt"), 0, 0
+        ),
+        axis=0,
+    )
     slot_values = tile_values[0, 0, 0]
     slot_tests = tile_test[0, 0, 0]
     slot_stmts = tile_stmt[0, 0, 0]

time: 510 us -> 403 us (0.79)
  blocking collectives: 402 us -> 71.5 us
  waiting for transfers between devices: 0.08 us -> 205 us
  starting transfers between devices: 0.05 us -> 15.1 us
    all_gather x1 -> x0, blocking collectives: 328 us -> none  [shards(): lax.all_gather(build_rows, ('test', 'stmt'), axis=0, tiled=True)]
    psum x1, waiting for transfers between devices: 0.02 us -> 164 us  [shards(): grams = lax.psum(local_grams, ALL)]
    reduce_scatter x1, waiting for transfers between devices: 0.03 us -> 41.1 us  [shards(): lax.psum_scatter(running_sum, ('build', 'test'), scatter_dimension=0, til...]
    all_to_all x0 -> x1, starting transfers between devices: none -> 15 us  [shards(): lax.all_to_all(jnp.stack([build_rows] * lax.axis_size(('test', 'stmt'))),...]
  transfers between devices with their start and end apart: 2 -> 3, of which waited for: 0 -> 2; matrix products, arithmetic and copies ran while one was open for 16% -> 16% of each run, Pallas kernels for 0% -> 0%
where the time goes in v1:
time: 403 us; the launch traced here: 402 us
  waiting for transfers between devices  205 us (51%)
  blocking collectives  71.5 us (18%)
  other arithmetic  57.4 us (14%)
  matrix products  21.8 us (5%)
  between operations  20.6 us (5%)
  starting transfers between devices  15.1 us (4%)
  local copies, waits for them, and re-layouts  10.9 us (3%)
    psum x1, waiting for transfers between devices, shards(): grams = lax.psum(local_grams, ALL)  164 us
    all_gather x1, blocking collectives, shards(): test_slab = lax.all_gather(test_rows, ('build', 'stmt'), axis=0, tiled=True)  71.5 us
    reduce_scatter x1, waiting for transfers between devices, shards(): lax.psum_scatter(running_sum, ('build', 'test'), scatter_dimension=0, til...  41.1 us
    another operation x6, other arithmetic, shards(): lower = jnp.linalg.cholesky(gram)  34 us
    another operation x3, other arithmetic, shards(): lax.linalg.triangular_solve(lower, owned_sums, left_side=False, lower=Tru...  19.7 us
    dot_general x2, matrix products, shards(): jnp.einsum('ijk,ikr->jr', slot_values[slot_index], khatri_rao, preferred_...  16.8 us
    all_to_all x1, starting transfers between devices, shards(): lax.all_to_all(jnp.stack([build_rows] * lax.axis_size(('test', 'stmt'))),...  15 us
  transfers between devices with their start and end apart: 3, of which 2 were waited for; matrix products, arithmetic and copies ran while one was open for 16% of the time, Pallas kernels for 0%

profile of v1, /device:TPU:32, one launch (start us, length us, event | category | flops | bytes accessed | tf_op | source)
XLA Modules:
  0.0 401.9 jit_solution(10253872871679277303)
XLA Ops:
  7.4 0.0 all-reduce.3.cloned.1.call-start
  7.4 1.0 convolution_bitcast_fusion
  8.4 1.0 convolution_bitcast_fusion.1
  9.4 0.8 pad_maximum_fusion
  10.2 0.0 all-reduce.3.cloned.1.call-update
  10.2 1.5 stack.12
  11.7 15.0 %all-to-all-start = ((bf16[128,6,256]{2,1,0:T(8,128)(2,1)}), bf16[128,6,256]{2,1,0:T(8,128)(2,1)S(1)}, u32[]{:S(2)}, u32[]{:S(2)}) async-start(bf16[128,6,256]{2,1,0:T(8,128)(2,1)} %stack.12), calls=%async_computation | async-start | bytes 1048576 | tf_op jit(solution)/shard_map/all_to_all | solution.py:29
  26.7 0.0 reduce-scatter.2.cloned.1.call-start
  26.8 1.4 fusion.53
  28.2 1.4 fusion.52
  29.6 1.4 fusion.54
  35.4 71.5 %all-gather = bf16[1,512,256]{2,1,0:T(8,128)(2,1)S(1)} all-gather(bf16[1,16,256]{2,1,0:T(8,128)(2,1)} %param.12), channel_id=2, replica_groups=mesh['build'=2,'test'=8,'stmt'=16] {'build','stmt'}, dimensions={1}, use_global_device_ids=true | all-gather | bytes 270336 | tf_op jit(solution)/shard_map/all_gather | solution.py:27
  106.9 163.6 %all-reduce.3.cloned.1.call-done = f32[2,256,256]{1,2,0:T(8,128)} async-done(((f32[2,256,256]{1,2,0:T(8,128)}), f32[2,256,256]{1,2,0:T(8,128)}) %all-reduce.3.cloned.1.call-update) | async-done | bytes 524304 | tf_op jit(solution)/shard_map/psum | solution.py:24
  270.5 1.1 fusion.38
  271.5 0.1 copy.20
  271.7 1.1 fusion.37
  272.8 11.7 %cholesky.49 = f32[128,128]{1,0:T(8,128)S(1)} custom-call(f32[128,128]{1,0:T(8,128)S(1)} %cholesky.115), custom_call_target="Cholesky" | custom-call | tf_op jit(solution)/shard_map/jit(cholesky)/cholesky | solution.py:26
  284.5 9.8 %custom-call.16 = f32[1,128,128]{1,2,0:T(8,128)S(1)} custom-call(f32[1,128,128]{2,1,0:T(8,128)S(1)} %get-tuple-element.30), custom_call_target="InvertDiagBlocksLowerTriangular" | custom-call | tf_op jit(solution)/shard_map/jit(cholesky)/cholesky | solution.py:26
  294.4 0.2 constant_dynamic-update-slice_fusion
  294.6 0.3 convolution_subtract_fusion
  294.9 11.7 %cholesky.103 = f32[128,128]{1,0:T(8,128)S(1)} custom-call(f32[128,128]{1,0:T(8,128)S(1)} %convolution_subtract_fusion), custom_call_target="Cholesky" | custom-call | tf_op jit(solution)/shard_map/jit(cholesky)/cholesky | solution.py:26
  306.6 0.7 compare_reduce_fusion
  308.5 0.0 all-to-all-done
  308.5 0.1 reshape.66
  308.7 0.1 copy.14
  308.8 0.1 copy.16
  308.9 8.5 %fusion.28 = f32[256,256]{1,0:T(8,128)S(1)} fusion(f32[256,256]{1,0:T(8,128)S(1)} %broadcast_in_dim.6, s32[]{:T(128)S(6)} %select_n.25, bf16[1,1,1,2,128,128,128]{6,5,4,3,2,1,0:T(8,128)(2,1)} %param.7, f32[128,256]{0,1:T(8,128)S(1)} %copy.14, f32[128,256]{1,0:T(8,128)S(1)} %get-tuple-element.26, f32[]{:T(128)} %bitcast.6), kind=kOutput, calls=%fused_computation.22 | convolution fusion | flops 1082163200 | bytes 4588036 | tf_op jit(solution)/shard_map/ijk,ikr->jr/dot_general | solution.py:50
  317.4 8.3 %fusion.34 = f32[256,256]{1,0:T(8,128)S(1)} fusion(f32[256,256]{1,0:T(8,128)S(1)} %fusion.28, s32[]{:T(128)S(6)} %select_n.26, bf16[1,1,1,2,128,128,128]{6,5,4,3,2,1,0:T(8,128)(2,1)} %param.7, f32[128,256]{0,1:T(8,128)S(1)} %copy.16, f32[128,256]{1,0:T(8,128)S(1)} %get-tuple-element.25, f32[]{:T(128)} %bitcast.15), kind=kOutput, calls=%fused_computation.24 | convolution fusion | flops 1082195968 | bytes 4719108 | tf_op jit(solution)/shard_map/ijk,ikr->jr/dot_general | solution.py:50
  325.7 0.0 copy-start
  325.7 0.7 copy-done
  326.4 0.0 reduce-scatter.2.cloned.1.call-update
  326.4 0.1 triangular_solve.67
  326.5 4.1 %while.1 = (s32[]{:T(128)}, f32[256,256]{1,0:T(8,128)S(1)}, s32[2,2]{1,0:T(2,128)S(1)}, f32[2,128,128]{2,1,0:T(8,128)S(1)}, s32[]{:T(128)}) while((s32[]{:T(128)}, f32[256,256]{1,0:T(8,128)S(1)}, s32[2,2]{1,0:T(2,128)S(1)}, f32[2,128,128]{2,1,0:T(8,128)S(1)}, s32[]{:T(128)}) %tuple.28), condition=%wide.while_cond, body=%wide.while_body.sunk | while | flops 2 | bytes 131181 | solution.py:61
  326.5 0.7 fusion.63
  327.2 1.3 bitcast_dynamic-update-slice_fusion.2
  328.5 0.7 fusion.63
  329.2 1.3 bitcast_dynamic-update-slice_fusion.2
  330.5 19.7 %custom-call.17 = f32[2,128,128]{1,2,0:T(8,128)S(1)} custom-call(f32[2,128,128]{2,1,0:T(8,128)S(1)} %get-tuple-element.12), custom_call_target="InvertDiagBlocksLowerTriangular" | custom-call | tf_op jit(solution)/shard_map/triangular_solve | solution.py:61
  350.2 41.1 %reduce-scatter.2.cloned.1.call-done = f32[16,256]{1,0:T(8,128)} async-done(((f32[256,256]{1,0:T(8,128)}), f32[16,256]{1,0:T(8,128)}) %reduce-scatter.2.cloned.1.call-update) | async-done | bytes 16400 | tf_op jit(solution)/shard_map/reduce_scatter | solution.py:60
  391.3 0.8 fusion.43
  392.1 0.9 convolution_subtract_fusion.2
  393.0 0.2 fusion.45
  393.2 0.2 fusion.44
  393.4 0.2 convolution_subtract_fusion.1
  393.6 0.2 fusion.42
  393.8 0.7 maximum_bitcast_fusion
  (12 shorter events, 0.2 us)
Async XLA Ops:
  7.4 263.1 %all-reduce.3.cloned.1.call-start = ((), (), s32[]{:S(2)}) async-start(), calls=%async_computation.3 | async-start | bytes 1048576 | tf_op jit(solution)/shard_map/psum | solution.py:24
  11.7 296.7 %all-to-all-start = ((bf16[128,6,256]{2,1,0:T(8,128)(2,1)}), bf16[128,6,256]{2,1,0:T(8,128)(2,1)S(1)}, u32[]{:S(2)}, u32[]{:S(2)}) async-start(bf16[128,6,256]{2,1,0:T(8,128)(2,1)} %stack.12), calls=%async_computation | async-start | bytes 1048576 | tf_op jit(solution)/shard_map/all_to_all | solution.py:29
  26.7 364.6 %reduce-scatter.2.cloned.1.call-start = ((), (), s32[]{:S(2)}) async-start(), calls=%async_computation.2 | async-start | bytes 278528 | tf_op jit(solution)/shard_map/reduce_scatter | solution.py:60
  325.7 0.7 copy-start
Sparse Core Ops, SparseCore 0:
  13.6 256.8 all-reduce.2
Sparse Core Ops, SparseCore 1:
  326.5 64.7 reduce-scatter.1
